TPU v7x, 256 devices: a whole 4x4x8 slice. The times are simulated.
256 devices in a mesh: prompt: 8 (over x, y_lo), tensor: 32 (over z, y_hi, core).
Axes of the slice: x: 4, y: 4 (y_hi: 2, y_lo: 2; y = y_hi * 2 + y_lo), z: 8, core: 2. Of those that a mesh axis runs over, the one named last changes fastest.
Arguments:
- tokens: bfloat16 [8, 128, 8192], P('prompt')
- gate_weight: bfloat16 [8192, 28672], P('prompt', 'tensor'), may hold values from -0.0625 to 0.0625
- up_weight: bfloat16 [8192, 28672], P('prompt', 'tensor'), may hold values from -0.0625 to 0.0625
- down_weight: bfloat16 [28672, 8192], P('tensor', 'prompt')
- norm_gain: float32 [8192], P('prompt'), may hold values from 0.1 to 1.9
- unembed: bfloat16 [8192, 86016], P('prompt', 'tensor'), may hold values from -0.5 to 0.5
- guidance: float32 [8], replicated, may hold values from -1.5 to 2.5
- logit_bias: float32 [128, 86016], P('prompt', 'tensor'), may hold values from -2 to 322
Outputs:
- log_probs: float32 [128, 86016], P('prompt', 'tensor')
All inputs are finite; a program needn't handle non-finite values.
Results may differ from a plain program's by a relative error of at most 0.0025.
Values may be sent and summed in bfloat16 or wider, within the bound.
No kernel may reach another device: no remote copies, remote signals or barrier semaphores. Data moves between devices by JAX's collectives and lax.ppermute only.
A program may use at most 64 MiB of HBM per device.

v0:
```python
import jax
import jax.numpy as jnp
from jax import lax
from jax.sharding import Mesh
from jax.sharding import PartitionSpec as P

D = 8192
PROMPT = ("prompt_0", "prompt_1")


def own_rows(so_far, axes):
    for axis in axes:
        so_far = lax.psum_scatter(so_far, axis, scatter_dimension=0, tiled=True)
    return so_far


def copy_for_each(array, axis):
    peers = lax.axis_size(axis)
    return lax.all_to_all(
        jnp.broadcast_to(array[None], (peers, *array.shape)), axis, 0, 0, tiled=True
    )


def joined_along(tiles, dim):
    tiles = jnp.moveaxis(tiles, 0, dim)
    shape = tiles.shape
    return tiles.reshape(*shape[:dim], shape[dim] * shape[dim + 1], *shape[dim + 2 :])


def collect(array, axis, dim):
    tiles = copy_for_each(array, axis)
    return joined_along(tiles, dim)


def of_everyone(array, axis):
    return copy_for_each(array, axis).sum(axis=0)


def cut_along(array, dim, peers):
    shape = array.shape
    tiles = array.reshape(*shape[:dim], peers, shape[dim] // peers, *shape[dim + 1 :])
    return jnp.moveaxis(tiles, dim, 0)


def sent_and_summed(array, axis, dim):
    tiles = cut_along(array, dim, lax.axis_size(axis))
    arrived = lax.all_to_all(tiles, axis, split_axis=0, concat_axis=0, tiled=True)
    return arrived.sum(axis=0)


def gathered_once(array, axis):
    leaves = jax.tree.leaves(array)
    turns = sorted(range(len(leaves)), key=lambda k: -leaves[k].size)
    width = (1, *leaves[turns[0]].shape)[-1]
    lines = [
        jnp.pad(leaves[k].reshape(-1), (0, -leaves[k].size % width)).reshape(-1, width)
        for k in turns
    ]
    both, at, found = (copy_for_each(jnp.concatenate(lines), axis), 0, {})
    for k, line in zip(turns, lines):
        slab = both[:, at : at + len(line)].reshape(len(both), -1)
        found[k] = slab[:, : leaves[k].size].reshape(-1, *leaves[k].shape)
        at += len(line)
    numbers = iter(range(len(leaves)))
    return jax.tree.map(lambda _: found[next(numbers)], array)


def combined_pairwise(pieces, combine):
    while len(jax.tree.leaves(pieces)[0]) > 1:
        pieces = jax.vmap(combine)(
            *(jax.tree.map(lambda part: part[side::2], pieces) for side in (0, 1))
        )
    return jax.tree.map(lambda part: part[0], pieces)


def merged(array, axis, combine):
    pieces = gathered_once(array, axis)
    return combined_pairwise(pieces, combine)


def combine_lse(first, second):
    top = jnp.maximum(first[0], second[0])
    total = first[1] * jnp.exp(first[0] - top) + second[1] * jnp.exp(second[0] - top)
    return (top, total)


def local(tokens, gate_weight, up_weight, down_weight, norm_gain, unembed, guidance, logit_bias):
    variants = lax.axis_size(PROMPT)
    rows = tokens.shape[1]
    share = gate_weight.shape[0]
    spread = lax.all_to_all(tokens, PROMPT, split_axis=2, concat_axis=0, tiled=True)
    flat = spread.reshape(variants * rows, share)
    gate_part = jnp.dot(flat, gate_weight, preferred_element_type=jnp.float32)
    up_part = jnp.dot(flat, up_weight, preferred_element_type=jnp.float32)
    gate_up = own_rows(jnp.concatenate([gate_part, up_part], axis=1), PROMPT)
    width = gate_weight.shape[1]
    hidden = (jax.nn.silu(gate_up[:, :width]) * gate_up[:, width:]).astype(jnp.bfloat16)
    partial_branch = jnp.dot(
        collect(hidden, PROMPT, 0), down_weight, preferred_element_type=jnp.float32
    )
    mine = lax.psum_scatter(partial_branch, "tensor", scatter_dimension=0, tiled=True)
    count = mine.shape[0]
    start = lax.axis_index("tensor") * count
    state = lax.dynamic_slice_in_dim(flat, start, count, 0).astype(jnp.float32) + mine
    square = of_everyone(jnp.sum(state * state, axis=1), PROMPT)
    owned = (state * lax.rsqrt(square / D + 1e-05)[:, None] * norm_gain).astype(jnp.bfloat16)
    normed = lax.all_gather(owned, "tensor", axis=0, tiled=True)
    blocks = normed.reshape(variants, rows, share)
    mixed = jnp.tensordot(guidance, blocks.astype(jnp.float32), axes=1)
    high = mixed.astype(jnp.bfloat16)
    low = (mixed - high.astype(jnp.float32)).astype(jnp.bfloat16)
    stacked = jnp.concatenate([high, low], axis=0)
    product = jnp.dot(stacked, unembed, preferred_element_type=jnp.float32)
    scores = (
        sent_and_summed(
            product[: rows // variants * lax.axis_size(PROMPT)]
            + product[rows // variants * lax.axis_size(PROMPT) :],
            PROMPT,
            0,
        )
        + logit_bias
    )
    local_top = jnp.max(scores, axis=1)
    local_total = jnp.sum(jnp.exp(scores - local_top[:, None]), axis=1)
    top, total_exp = merged((local_top, local_total), "tensor", combine_lse)
    return scores - top[:, None] - jnp.log(total_exp)[:, None]


def solution(mesh):
    finer = Mesh(
        mesh.devices.reshape(4, 2, mesh.shape["tensor"]), ("prompt_0", "prompt_1", "tensor")
    )
    placed = (
        P(PROMPT, None, None),
        P(PROMPT, "tensor"),
        P(PROMPT, "tensor"),
        P("tensor", PROMPT),
        P(PROMPT),
        P(PROMPT, "tensor"),
        P(),
        P(PROMPT, "tensor"),
    )
    return jax.shard_map(
        local, mesh=finer, in_specs=placed, out_specs=P(PROMPT, "tensor"), check_vma=False
    )
```

profile of v0, /device:TPU:1, one launch (start us, length us, event | category | flops | bytes accessed | tf_op | source)
XLA Modules:
  0.0 547.3 jit_solution(13178497889290529071)
XLA Ops:
  6.5 9.6 %copy.23 = bf16[1,128,8192]{1,0,2:T(2,128)(2,1)} copy(bf16[1,128,8192]{2,1,0:T(8,128)(2,1)} %param.8) | data formatting | bytes 4194304 | tf_op args[0]
  16.7 46.5 %reduce.1 = bf16[8192,128]{1,0:T(8,128)(2,1)} reduce(bf16[8192,1,128]{2,1,0:T(2,128)(2,1)} %bitcast.47, bf16[]{:T(256)} %broadcast.18), dimensions={1}, to_apply=%bitcast.29.reduce_sub_computation | reduce | bytes 4194306
  63.2 5.8 %reshape.57 = bf16[8,2,65536]{2,1,0:T(2,128)(2,1)} reshape(bf16[8192,128]{1,0:T(8,128)(2,1)} %reduce.1) | data formatting | bytes 4194304
  69.0 31.1 %all_to_all.36 = bf16[8,2,65536]{2,1,0:T(2,128)(2,1)} all-to-all(bf16[8,2,65536]{2,1,0:T(2,128)(2,1)} %reshape.57), channel_id=1, replica_groups=mesh['prompt_0'=4,'prompt_1'=2,'tensor'=32] {'prompt_0','prompt_1'}, dimensions={0} | all-to-all | bytes 4194304 | tf_op jit(solution)/shard_map/all_to_all | solution.py:91
  100.1 6.8 %reshape.58 = bf16[8192,1,128]{2,1,0:T(2,128)(2,1)} reshape(bf16[8,2,65536]{2,1,0:T(2,128)(2,1)} %all_to_all.36) | data formatting | bytes 4194304
  106.8 3.8 copy.30
  110.6 4.0 copy.24
  114.6 4.5 fusion.15
  119.1 2.2 fusion.16
  121.3 3.7 pad_maximum_fusion
  125.0 78.3 %reduce-scatter.4.cloned.1.call-done = f32[256,1792]{0,1:T(8,128)} async-done(((f32[1024,1792]{0,1:T(8,128)}), f32[256,1792]{0,1:T(8,128)}) %reduce-scatter.4.cloned.1.call-update) | async-done | bytes 1835024 | tf_op jit(solution)/shard_map/reduce_scatter | solution.py:13
  203.6 36.1 %reduce-scatter.6.cloned.1.call-done = f32[128,1792]{0,1:T(8,128)} async-done(((f32[256,1792]{0,1:T(8,128)}), f32[128,1792]{0,1:T(8,128)}) %reduce-scatter.6.cloned.1.call-update) | async-done | bytes 917520 | tf_op jit(solution)/shard_map/reduce_scatter | solution.py:13
  239.7 1.3 fusion.7
  241.4 26.5 %all_to_all.37 = bf16[8,128,896]{2,1,0:T(8,128)(2,1)S(1)} all-to-all(bf16[8,128,896]{2,1,0:T(8,128)(2,1)S(1)} %broadcast_in_dim.6), channel_id=1, replica_groups=mesh['prompt_0'=4,'prompt_1'=2,'tensor'=32] {'prompt_0','prompt_1'}, dimensions={0} | all-to-all | bytes 3670016 | tf_op jit(solution)/shard_map/all_to_all | solution.py:19
  267.9 4.3 fusion.17
  272.3 124.4 %reduce-scatter.8.cloned.1.call-done = f32[32,1024]{1,0:T(8,128)} async-done(((f32[1024,1024]{1,0:T(8,128)}), f32[32,1024]{1,0:T(8,128)}) %reduce-scatter.8.cloned.1.call-update) | async-done | bytes 131088 | tf_op jit(solution)/shard_map/reduce_scatter | solution.py:101
  396.6 1.0 multiply_reduce_fusion
  397.7 9.7 %all_to_all.38 = f32[8,1,32]{2,1,0:T(1,128)S(1)} all-to-all(f32[8,1,32]{2,1,0:T(1,128)S(1)} %broadcast_in_dim.7), channel_id=1, replica_groups=mesh['prompt_0'=4,'prompt_1'=2,'tensor'=32] {'prompt_0','prompt_1'}, dimensions={0} | all-to-all | bytes 2048 | tf_op jit(solution)/shard_map/all_to_all | solution.py:19
  407.4 1.6 multiply_convert_fusion
  409.0 83.2 %all-gather.2.cloned.1.call-done = bf16[1024,1024]{1,0:T(8,128)(2,1)} async-done(((bf16[32,1024]{1,0:T(8,128)(2,1)}), bf16[1024,1024]{1,0:T(8,128)(2,1)}) %all-gather.2.cloned.1.call-update) | async-done | bytes 2097168 | tf_op jit(solution)/shard_map/all_gather | solution.py:107
  492.3 3.0 fusion
  495.5 4.2 fusion.2
  499.9 22.2 %all_to_all.39 = f32[8,16,2688]{2,1,0:T(8,128)S(1)} all-to-all(f32[8,16,2688]{2,1,0:T(8,128)S(1)} %bitcast.50), channel_id=1, replica_groups=mesh['prompt_0'=4,'prompt_1'=2,'tensor'=32] {'prompt_0','prompt_1'}, dimensions={0} | all-to-all | bytes 2752512 | tf_op jit(solution)/shard_map/all_to_all | solution.py:47
  522.5 17.0 %all_to_all.40 = f32[32,2,16]{2,1,0:T(2,128)S(1)} all-to-all(f32[32,2,16]{2,1,0:T(2,128)S(1)} %broadcast_in_dim.8), channel_id=1, replica_groups=mesh['prompt_0'=4,'prompt_1'=2,'tensor'=32] {'tensor'}, dimensions={0} | all-to-all | bytes 8192 | tf_op jit(solution)/shard_map/all_to_all | solution.py:19
  (57 shorter events, 3.3 us)
Async XLA Ops:
  6.5 261.4 %copy-start = (bf16[896,1024]{1,0:T(8,128)(2,1)S(1)}, bf16[896,1024]{1,0:T(8,128)(2,1)}, u32[]{:S(2)}) copy-start(bf16[896,1024]{1,0:T(8,128)(2,1)} %param.11) | copy-start | bytes 5505028
  6.5 196.8 %reduce-scatter.4.cloned.1.call-start = ((), (), s32[]{:S(2)}) async-start(), calls=%async_computation.8 | async-start | bytes 9175040 | tf_op jit(solution)/shard_map/reduce_scatter | solution.py:13
  114.6 4.5 copy-start.1
  114.6 4.5 copy-start.5
  125.0 114.7 %reduce-scatter.6.cloned.1.call-start = ((), (), s32[]{:S(2)}) async-start(), calls=%async_computation.9 | async-start | bytes 2752512 | tf_op jit(solution)/shard_map/reduce_scatter | solution.py:13
  203.4 193.3 %reduce-scatter.8.cloned.1.call-start = ((), (), s32[]{:S(2)}) async-start(), calls=%async_computation.10 | async-start | bytes 4325376 | tf_op jit(solution)/shard_map/reduce_scatter | solution.py:101
  272.2 135.2 %copy-start.3 = (f32[1024]{0:T(1024)S(1)}, f32[1024]{0:T(1024)}, u32[]{:S(2)}) copy-start(f32[1024]{0:T(1024)} %param.12) | copy-start | bytes 12292
  272.2 220.1 %copy-start.4 = (f32[8]{0:T(128)S(1)}, f32[8]{0:T(128)}, u32[]{:S(2)}) copy-start(f32[8]{0:T(128)} %param.14) | copy-start | bytes 100
  272.2 220.1 %all-gather.2.cloned.1.call-start = ((), (), s32[]{:S(2)}) async-start(), calls=%async_computation.11 | async-start | bytes 2162688 | tf_op jit(solution)/shard_map/all_gather | solution.py:107
  499.8 22.3 %copy-start.2 = (f32[16,2688]{1,0:T(8,128)S(1)}, f32[16,2688]{1,0:T(8,128)}, u32[]{:S(2)}) copy-start(f32[16,2688]{1,0:T(8,128)} %param.15) | copy-start | bytes 516100
Sparse Core Ops, SparseCore 0:
  125.1 78.1 reduce-scatter.3
  205.8 33.7 reduce-scatter.5
  272.3 124.2 reduce-scatter.7
  409.1 83.0 all-gather.1
where the time goes:
time: 548 us; the launch traced here: 547 us
  waiting for transfers between devices  322 us (59%)
  blocking collectives  106 us (19%)
  other arithmetic  55.7 us (10%)
  local copies, waits for them, and re-layouts  31.3 us (6%)
  matrix products  18.1 us (3%)
  between operations  13.3 us (2%)
    reduce_scatter x1, waiting for transfers between devices, local(): lax.psum_scatter(partial_branch, 'tensor', scatter_dimension=0, tiled=True)  124 us
    reduce_scatter x2, waiting for transfers between devices, own_rows(): so_far = lax.psum_scatter(so_far, axis, scatter_dimension=0, tiled=True)  114 us
    all_gather x1, waiting for transfers between devices, local(): normed = lax.all_gather(owned, 'tensor', axis=0, tiled=True)  83.2 us
    all_to_all x3, blocking collectives, copy_for_each(): lax.all_to_all(jnp.broadcast_to(array[None], (peers, *array.shape)), axis...  53.2 us
    unnamed x1, other arithmetic  46.5 us
    all_to_all x1, blocking collectives, local(): lax.all_to_all(tokens, PROMPT, split_axis=2, concat_axis=0, tiled=True)  31.1 us
    unnamed x17, local copies, waits for them, and re-layouts  26.5 us
    all_to_all x1, blocking collectives, sent_and_summed(): lax.all_to_all(tiles, axis, split_axis=0, concat_axis=0, tiled=True)  22.2 us
  transfers between devices with their start and end apart: 4, of which 4 were waited for; matrix products, arithmetic and copies ran while one was open for 0% of the time, Pallas kernels for 0%

commit v1 on v0

--- a/solution.py
+++ b/solution.py
@@ -88,7 +88,10 @@
     variants = lax.axis_size(PROMPT)
     rows = tokens.shape[1]
     share = gate_weight.shape[0]
-    spread = lax.all_to_all(tokens, PROMPT, split_axis=2, concat_axis=0, tiled=True)
+    spread = jnp.concatenate(
+        lax.all_to_all(jnp.stack(jnp.split(tokens, lax.axis_size(PROMPT), axis=2)), PROMPT, 0, 0),
+        axis=0,
+    )
     flat = spread.reshape(variants * rows, share)
     gate_part = jnp.dot(flat, gate_weight, preferred_element_type=jnp.float32)
     up_part = jnp.dot(flat, up_weight, preferred_element_type=jnp.float32)

time: 548 us -> 477 us (0.87)
  other arithmetic: 55.7 us -> 9.15 us
  local copies, waits for them, and re-layouts: 31.3 us -> 8.81 us
    unnamed x1 -> x0, other arithmetic: 46.5 us -> none
    unnamed x17 -> x21, local copies, waits for them, and re-layouts: 26.5 us -> 7.01 us
where the time goes in v1:
time: 477 us; the launch traced here: 476 us
  waiting for transfers between devices  322 us (68%)
  blocking collectives  106 us (22%)
  matrix products  15.9 us (3%)
  between operations  13.3 us (3%)
  other arithmetic  9.15 us (2%)
  local copies, waits for them, and re-layouts  8.81 us (2%)
    reduce_scatter x1, waiting for transfers between devices, local(): lax.psum_scatter(partial_branch, 'tensor', scatter_dimension=0, tiled=True)  125 us
    reduce_scatter x2, waiting for transfers between devices, own_rows(): so_far = lax.psum_scatter(so_far, axis, scatter_dimension=0, tiled=True)  114 us
    all_gather x1, waiting for transfers between devices, local(): normed = lax.all_gather(owned, 'tensor', axis=0, tiled=True)  83.6 us
    all_to_all x3, blocking collectives, copy_for_each(): lax.all_to_all(jnp.broadcast_to(array[None], (peers, *array.shape)), axis...  52.6 us
    all_to_all x1, blocking collectives, local(): lax.all_to_all(jnp.stack(jnp.split(tokens, lax.axis_size(PROMPT), axis=2)...  31.6 us
    all_to_all x1, blocking collectives, sent_and_summed(): lax.all_to_all(tiles, axis, split_axis=0, concat_axis=0, tiled=True)  22.2 us
  transfers between devices with their start and end apart: 4, of which 4 were waited for; matrix products, arithmetic and copies ran while one was open for 0% of the time, Pallas kernels for 0%

profile of v1, /device:TPU:1, one launch (start us, length us, event | category | flops | bytes accessed | tf_op | source)
XLA Modules:
  0.0 475.9 jit_solution(11970162396997846273)
XLA Ops:
  6.5 1.1 bitcast_dynamic-update-slice_fusion.7
  7.6 1.0 bitcast_dynamic-update-slice_fusion.6
  8.6 1.0 bitcast_dynamic-update-slice_fusion.5
  9.6 1.0 bitcast_dynamic-update-slice_fusion.4
  10.6 1.0 bitcast_dynamic-update-slice_fusion.3
  12.5 1.0 bitcast_dynamic-update-slice_fusion.1
  14.5 31.6 %all_to_all.26 = bf16[8,1,128,1024]{3,2,1,0:T(8,128)(2,1)S(1)} all-to-all(bf16[8,1,128,1024]{3,2,1,0:T(8,128)(2,1)S(1)} %bitcast_dynamic-update-slice_fusion), channel_id=1, replica_groups=mesh['prompt_0'=4,'prompt_1'=2,'tensor'=32] {'prompt_0','prompt_1'}, dimensions={0} | all-to-all | bytes 4194304 | tf_op jit(solution)/shard_map/all_to_all | solution.py:92
  46.0 2.2 fusion.15
  48.3 2.2 fusion.16
  50.5 3.7 pad_maximum_fusion
  54.2 77.6 %reduce-scatter.4.cloned.1.call-done = f32[256,1792]{0,1:T(8,128)} async-done(((f32[1024,1792]{0,1:T(8,128)}), f32[256,1792]{0,1:T(8,128)}) %reduce-scatter.4.cloned.1.call-update) | async-done | bytes 1835024 | tf_op jit(solution)/shard_map/reduce_scatter | solution.py:13
  131.9 36.3 %reduce-scatter.6.cloned.1.call-done = f32[128,1792]{0,1:T(8,128)} async-done(((f32[256,1792]{0,1:T(8,128)}), f32[128,1792]{0,1:T(8,128)}) %reduce-scatter.6.cloned.1.call-update) | async-done | bytes 917520 | tf_op jit(solution)/shard_map/reduce_scatter | solution.py:13
  168.2 1.3 fusion.7
  169.9 26.3 %all_to_all.27 = bf16[8,128,896]{2,1,0:T(8,128)(2,1)S(1)} all-to-all(bf16[8,128,896]{2,1,0:T(8,128)(2,1)S(1)} %broadcast_in_dim.6), channel_id=1, replica_groups=mesh['prompt_0'=4,'prompt_1'=2,'tensor'=32] {'prompt_0','prompt_1'}, dimensions={0} | all-to-all | bytes 3670016 | tf_op jit(solution)/shard_map/all_to_all | solution.py:19
  196.2 4.3 fusion.17
  200.5 124.7 %reduce-scatter.8.cloned.1.call-done = f32[32,1024]{1,0:T(8,128)} async-done(((f32[1024,1024]{1,0:T(8,128)}), f32[32,1024]{1,0:T(8,128)}) %reduce-scatter.8.cloned.1.call-update) | async-done | bytes 131088 | tf_op jit(solution)/shard_map/reduce_scatter | solution.py:104
  325.2 1.0 multiply_reduce_fusion
  326.3 9.3 %all_to_all.28 = f32[8,1,32]{2,1,0:T(1,128)S(1)} all-to-all(f32[8,1,32]{2,1,0:T(1,128)S(1)} %broadcast_in_dim.7), channel_id=1, replica_groups=mesh['prompt_0'=4,'prompt_1'=2,'tensor'=32] {'prompt_0','prompt_1'}, dimensions={0} | all-to-all | bytes 2048 | tf_op jit(solution)/shard_map/all_to_all | solution.py:19
  335.6 1.6 multiply_convert_fusion
  337.2 83.6 %all-gather.2.cloned.1.call-done = bf16[1024,1024]{1,0:T(8,128)(2,1)} async-done(((bf16[32,1024]{1,0:T(8,128)(2,1)}), bf16[1024,1024]{1,0:T(8,128)(2,1)}) %all-gather.2.cloned.1.call-update) | async-done | bytes 2097168 | tf_op jit(solution)/shard_map/all_gather | solution.py:110
  420.9 3.0 fusion
  424.1 4.2 fusion.2
  428.5 22.2 %all_to_all.29 = f32[8,16,2688]{2,1,0:T(8,128)S(1)} all-to-all(f32[8,16,2688]{2,1,0:T(8,128)S(1)} %bitcast.58), channel_id=1, replica_groups=mesh['prompt_0'=4,'prompt_1'=2,'tensor'=32] {'prompt_0','prompt_1'}, dimensions={0} | all-to-all | bytes 2752512 | tf_op jit(solution)/shard_map/all_to_all | solution.py:47
  451.1 17.0 %all_to_all.30 = f32[32,2,16]{2,1,0:T(2,128)S(1)} all-to-all(f32[32,2,16]{2,1,0:T(2,128)S(1)} %broadcast_in_dim.8), channel_id=1, replica_groups=mesh['prompt_0'=4,'prompt_1'=2,'tensor'=32] {'tensor'}, dimensions={0} | all-to-all | bytes 8192 | tf_op jit(solution)/shard_map/all_to_all | solution.py:19
  (60 shorter events, 4.6 us)
Async XLA Ops:
  6.5 189.6 %copy-start = (bf16[896,1024]{1,0:T(8,128)(2,1)S(1)}, bf16[896,1024]{1,0:T(8,128)(2,1)}, u32[]{:S(2)}) copy-start(bf16[896,1024]{1,0:T(8,128)(2,1)} %param.11) | copy-start | bytes 5505028
  6.5 125.3 %reduce-scatter.4.cloned.1.call-start = ((), (), s32[]{:S(2)}) async-start(), calls=%async_computation.8 | async-start | bytes 9175040 | tf_op jit(solution)/shard_map/reduce_scatter | solution.py:13
  14.5 31.6 %copy-start.5 = (bf16[1024,896]{1,0:T(8,128)(2,1)S(1)}, bf16[1024,896]{1,0:T(8,128)(2,1)}, u32[]{:S(2)}) copy-start(bf16[1024,896]{1,0:T(8,128)(2,1)} %param.9) | copy-start | bytes 5505028
  46.0 2.2 copy-start.1
  46.0 2.3 copy-start.6
  54.2 114.0 %reduce-scatter.6.cloned.1.call-start = ((), (), s32[]{:S(2)}) async-start(), calls=%async_computation.9 | async-start | bytes 2752512 | tf_op jit(solution)/shard_map/reduce_scatter | solution.py:13
  131.9 193.3 %reduce-scatter.8.cloned.1.call-start = ((), (), s32[]{:S(2)}) async-start(), calls=%async_computation.10 | async-start | bytes 4325376 | tf_op jit(solution)/shard_map/reduce_scatter | solution.py:104
  200.4 135.1 %copy-start.3 = (f32[1024]{0:T(1024)S(1)}, f32[1024]{0:T(1024)}, u32[]{:S(2)}) copy-start(f32[1024]{0:T(1024)} %param.12) | copy-start | bytes 12292
  200.5 220.4 %copy-start.4 = (f32[8]{0:T(128)S(1)}, f32[8]{0:T(128)}, u32[]{:S(2)}) copy-start(f32[8]{0:T(128)} %param.14) | copy-start | bytes 100
  200.5 220.4 %all-gather.2.cloned.1.call-start = ((), (), s32[]{:S(2)}) async-start(), calls=%async_computation.11 | async-start | bytes 2162688 | tf_op jit(solution)/shard_map/all_gather | solution.py:110
  428.5 22.3 %copy-start.2 = (f32[16,2688]{1,0:T(8,128)S(1)}, f32[16,2688]{1,0:T(8,128)}, u32[]{:S(2)}) copy-start(f32[16,2688]{1,0:T(8,128)} %param.15) | copy-start | bytes 516100
Sparse Core Ops, SparseCore 0:
  54.3 77.4 reduce-scatter.3
  134.3 33.7 reduce-scatter.5
  200.6 124.5 reduce-scatter.7
  337.4 83.4 all-gather.1
